TPU v7x, 32 devices: a whole 2x2x4 slice. The times are simulated.
32 devices in a mesh: groups: 2 (over x), vel: 16 (over z, y, core).
Axes of the slice: x: 2, y: 2, z: 4, core: 2. Of those that a mesh axis runs over, the one named last changes fastest.
Arguments:
- signal: bfloat16 [32, 8, 512], P(('groups', 'vel')), parts along dimension 0, may hold values from -6 to 6
- weight: bfloat16 [32, 8, 512], P(('groups', 'vel')), parts along dimension 0, may hold values from 0.25 to 4
- shifts: int32 [16, 16, 2], P('vel'), may hold values from -15 to 15, as said below
- phases: int32 [16, 16, 2], P('vel'), may hold values from 0 to 7, as said below
Outputs:
- likelihood: float32 [32, 8, 512], P(('groups', 'vel')), parts along dimension 0
- best_likelihood: float32 [16, 512], P('groups'), parts along dimension 0
There are 2 independent parts, one for each index of `groups`. A program takes and returns all parts, laid end to end along the dimension named above; an argument that names none is the same for every part. Nothing has to cross between parts.
Inputs may be any that keep to these rules, and one draw needn't show every extreme that they name: shifts[v, e] = floor(o / 8) of offsets o in eighths of a pixel that grow with the exposure index e for each velocity: column offset a_v e with a_v in -8..8, row offset floor(b_v e / 16) with b_v in -8..8; some velocity has a_v = 8 and another a_v = -8. phases[v, e] = the same offsets modulo 8.
All inputs are finite; a program needn't handle non-finite values.
Results may differ from a plain program's by a relative error of at most 0.0003.
Values may be sent and summed in bfloat16 or wider, within the bound.
A program may use at most 64 MiB of HBM per device.

v0:
```python
import jax
import jax.numpy as jnp
from jax import lax
from jax.sharding import PartitionSpec as P


def tap_table():
    fraction = jnp.arange(8, dtype=jnp.float32) / 8.0
    position = (jnp.arange(6, dtype=jnp.int32) - 2).astype(jnp.float32)
    distance = position[None, :] - fraction[:, None]
    raw_taps = jnp.sinc(distance) * jnp.sinc(distance / 3.0)
    return (raw_taps / jnp.sum(raw_taps, axis=1, keepdims=True)).astype(jnp.float32)


def pick_taps(coefficients, phase_index):
    choose = (jnp.arange(coefficients.shape[0], dtype=jnp.int32) == phase_index).astype(jnp.float32)
    return jnp.sum(choose[:, None] * coefficients, axis=0)


def place_pair(padded, shift_pair, phase_pair, coefficients, margin, columns, reach):
    height = padded.shape[1]
    col_taps = pick_taps(coefficients, phase_pair[1])
    row_taps = pick_taps(coefficients, phase_pair[0])
    anchor = shift_pair[0] * 0
    col_start = reach + shift_pair[1] - 2
    slab = lax.dynamic_slice(padded, (anchor, anchor, col_start), (2, height, columns + 5)).astype(
        jnp.float32
    )
    row_pass = sum(
        (
            col_taps[tap_index] * slab[:, :, tap_index : tap_index + columns]
            for tap_index in range(6)
        )
    )
    tall = jnp.pad(row_pass, ((0, 0), (margin, margin), (0, 0)))
    row_start = margin + shift_pair[0] - 2
    slab_rows = lax.dynamic_slice(tall, (anchor, row_start, anchor), (2, height + 5, columns))
    return sum(
        (
            row_taps[tap_index] * slab_rows[:, tap_index : tap_index + height, :]
            for tap_index in range(6)
        )
    )


def place_block(padded, shift_block, phase_block, coefficients, margin, columns, reach):
    placed = jax.vmap(
        lambda image, shift_pair, phase_pair: place_pair(
            image, shift_pair, phase_pair, coefficients, margin, columns, reach
        )
    )(padded, shift_block, phase_block)
    return jnp.sum(placed, axis=0)


def stack_velocities(padded, shift_rows, phase_rows, coefficients, margin, columns, reach):
    count = padded.shape[0]
    height = padded.shape[2]
    block = 32 if count % 32 == 0 else count
    groups_count = count // block

    def one_velocity(inputs):
        shift_set, phase_set = inputs
        if groups_count == 1:
            return place_block(padded, shift_set, phase_set, coefficients, margin, columns, reach)
        blocked = padded.reshape((groups_count, block) + padded.shape[1:])
        shift_blocks = shift_set.reshape((groups_count, block, 2))
        phase_blocks = phase_set.reshape((groups_count, block, 2))

        def add_block(total, item):
            images, shift_block, phase_block = item
            return (
                total
                + place_block(
                    images, shift_block, phase_block, coefficients, margin, columns, reach
                ),
                None,
            )

        start = jnp.zeros((2, height, columns), jnp.float32)
        total, unused = lax.scan(add_block, start, (blocked, shift_blocks, phase_blocks))
        return total

    return lax.map(one_velocity, (shift_rows, phase_rows))


def widen(signal_part, weight_part, reach):
    images = jnp.stack([signal_part, weight_part], axis=1)
    return jnp.pad(images, ((0, 0), (0, 0), (0, 0), (reach, reach)))


def body(signal, weight, shifts, phases):
    coefficients = tap_table()
    columns = signal.shape[2]
    margin = shifts.shape[1] // 16 + 6
    reach = shifts.shape[1] + 3
    gathered_signal, gathered_weight = (
        lax.all_gather(signal, "vel", axis=0, tiled=True),
        lax.all_gather(weight, "vel", axis=0, tiled=True),
    )
    summed = stack_velocities(
        widen(gathered_signal, gathered_weight, reach),
        shifts,
        phases,
        coefficients,
        margin,
        columns,
        reach,
    )
    likelihood = summed[:, 0] / jnp.sqrt(jnp.maximum(summed[:, 1], 1.0))
    best_likelihood = lax.pmax(jnp.max(likelihood, axis=0), "vel")
    return (likelihood, best_likelihood)


def solution(mesh):
    in_specs = (
        P(("groups", "vel"), None, None),
        P(("groups", "vel"), None, None),
        P("vel", None, None),
        P("vel", None, None),
    )
    out_specs = (P(("groups", "vel"), None, None), P("groups", None))
    return jax.shard_map(body, mesh=mesh, in_specs=in_specs, out_specs=out_specs, check_vma=False)
```

profile of v0, /device:TPU:0, one launch (start us, length us, event | category | flops | bytes accessed | tf_op | source)
XLA Modules:
  0.0 174.9 jit_solution(8193985154500921316)
XLA Ops:
  0.6 23.7 %all_gather.7 = bf16[16,8,512]{2,1,0:T(8,128)(2,1)S(1)} all-gather(bf16[1,8,512]{2,1,0:T(8,128)(2,1)} %param.6), channel_id=1, replica_groups=mesh['groups'=2,'vel'=16] {'vel'}, dimensions={0}, use_global_device_ids=true | all-gather | bytes 139264 | tf_op jit(solution)/shard_map/all_gather | solution.py:98
  24.3 7.5 %copy.24 = bf16[16,1,8,512]{2,1,0,3:T(2,128)(2,1)} copy(bf16[16,1,8,512]{3,2,0,1:T(8,128)(2,1)S(1)} %bitcast.42) | data formatting | bytes 262144 | tf_op jit(solution)/shard_map/stack | solution.py:87
  31.9 18.0 %all_gather.6 = bf16[16,8,512]{2,1,0:T(8,128)(2,1)S(1)} all-gather(bf16[1,8,512]{2,1,0:T(8,128)(2,1)} %param.5), channel_id=1, replica_groups=mesh['groups'=2,'vel'=16] {'vel'}, dimensions={0}, use_global_device_ids=true | all-gather | bytes 139264 | tf_op jit(solution)/shard_map/all_gather | solution.py:97
  49.9 7.5 %copy.23 = bf16[16,1,8,512]{2,1,0,3:T(2,128)(2,1)} copy(bf16[16,1,8,512]{3,2,0,1:T(8,128)(2,1)S(1)} %bitcast.43) | data formatting | bytes 262144 | tf_op jit(solution)/shard_map/stack | solution.py:87
  57.4 0.0 copy-start
  57.4 28.2 %select_maximum_fusion = bf16[16,2,8,550]{2,1,0,3:T(2,128)(2,1)} fusion(bf16[16,1,8,512]{2,1,0,3:T(2,128)(2,1)} %copy.24, bf16[16,1,8,512]{2,1,0,3:T(2,128)(2,1)} %copy.23), kind=kLoop, calls=%fused_computation.3 | loop fusion | flops 1267200 | bytes 543744 | tf_op jit(solution)/shard_map/stack | solution.py:87
  85.6 0.0 copy-start.1
  85.6 0.0 copy-done
  85.6 15.2 %gather_fusion = bf16[16,2,8,517]{2,1,3,0:T(2,128)(2,1)} fusion(bf16[16,2,8,550]{2,1,0,3:T(2,128)(2,1)} %select_maximum_fusion, s32[16]{0:T(128)S(1)} %get-tuple-element.42), kind=kCustom, calls=%fused_computation | custom fusion | bytes 529664 | tf_op jit(solution)/shard_map/while/body/eval_jaxpr/vmap()/gather | solution.py:26
  100.8 9.2 %copy.25 = bf16[16,2,8,517]{3,2,1,0:T(8,128)(2,1)S(1)} copy(bf16[16,2,8,517]{2,1,3,0:T(2,128)(2,1)} %gather_fusion) | data formatting | bytes 529408 | tf_op jit(solution)/shard_map/while/body/eval_jaxpr/vmap()/gather | solution.py:26
  110.0 0.1 convert_element_type.40
  110.1 0.2 fusion.58
  110.3 0.1 broadcast_divide_fusion
  110.4 0.1 copy.22
  110.5 0.0 copy-done.1
  110.5 0.1 multiply_reduce_fusion.1
  110.6 0.9 fusion.5
  111.5 0.4 copy.29
  111.9 0.5 pad.11.clone
  112.4 1.5 gather_fusion.1
  113.9 1.2 fusion.10
  115.2 0.6 copy.27
  115.8 59.1 %pmax.7 = f32[8,512]{1,0:T(8,128)} all-reduce(f32[8,512]{1,0:T(8,128)S(1)} %bitcast.46), channel_id=1, replica_groups=mesh['groups'=2,'vel'=16] {'vel'}, use_global_device_ids=true, to_apply=%region_4.6 | all-reduce | flops 4096 | bytes 32768 | tf_op jit(solution)/shard_map/pmax | solution.py:110
  (10 shorter events, 0.1 us)
Async XLA Ops:
  57.4 28.2 %copy-start = (s32[1,16,2]{1,2,0:T(2,128)S(1)}, s32[1,16,2]{1,2,0:T(2,128)}, u32[]{:S(2)}) copy-start(s32[1,16,2]{1,2,0:T(2,128)} %param.7) | copy-start | bytes 388
  85.6 24.9 %copy-start.1 = (s32[1,16,2]{1,2,0:T(2,128)S(1)}, s32[1,16,2]{1,2,0:T(2,128)}, u32[]{:S(2)}) copy-start(s32[1,16,2]{1,2,0:T(2,128)} %param.8) | copy-start | bytes 388
where the time goes:
time: 175 us
  blocking collectives  101 us (58%)
  local copies, waits for them, and re-layouts  42.5 us (24%)
  other arithmetic  30.8 us (18%)
    pmax x1, blocking collectives, body(): best_likelihood = lax.pmax(jnp.max(likelihood, axis=0), 'vel')  59.1 us
    another operation x1, other arithmetic, widen(): images = jnp.stack([signal_part, weight_part], axis=1)  28.2 us
    gather x2, local copies, waits for them, and re-layouts, place_pair(): lax.dynamic_slice(padded, (anchor, anchor, col_start), (2, height, column...  24.4 us
    all_gather x1, blocking collectives, body(): lax.all_gather(weight, 'vel', axis=0, tiled=True)  23.7 us
    all_gather x1, blocking collectives, body(): lax.all_gather(signal, 'vel', axis=0, tiled=True)  18 us
    another operation x2, local copies, waits for them, and re-layouts, widen(): images = jnp.stack([signal_part, weight_part], axis=1)  15 us

commit v1 on v0

v1 whole, which is shorter than its diff:
```python
import functools
import math

import jax
import jax.numpy as jnp
import numpy as np
from jax import lax
from jax.experimental import pallas as pl
from jax.experimental.pallas import tpu as pltpu
from jax.sharding import PartitionSpec as P

TAPS = 6
PHASES = 8
LANES = 128
MESH = pl.DeviceIdType.MESH


def tap_table():
    distance = (np.arange(TAPS)[None, :] - 2) - np.arange(PHASES)[:, None] / 8.0
    raw = np.sinc(distance) * np.sinc(distance / 3.0)
    return (raw / raw.sum(axis=1, keepdims=True)).astype(np.float32)


def loop(start, stop, step):
    if stop - start <= 16:
        for at in range(start, stop):
            step(at)
    else:
        lax.fori_loop(start, stop, lambda at, c: (step(at), c)[1], 0)


def pick_phase(phase, column):
    value = jnp.full(phase.shape, float(column[0]), jnp.float32)
    for at in range(1, PHASES):
        value = jnp.where(phase == at, float(column[at]), value)
    return value


def coefficient_rows(shifts_ref, phases_ref, exposures, height):
    depth = exposures * 2 * height
    table = tap_table()
    lane = lax.broadcasted_iota(jnp.int32, (1, depth), 1)
    owner = lane // (2 * height)

    def spread(e, held):
        row_shift, row_phase, col_phase = held
        here = owner == e
        return (
            jnp.where(here, shifts_ref[0, e, 0], row_shift),
            jnp.where(here, phases_ref[0, e, 0], row_phase),
            jnp.where(here, phases_ref[0, e, 1], col_phase),
        )

    held = (jnp.zeros((1, depth), jnp.int32),) * 3
    if exposures <= 16:
        for e in range(exposures):
            held = spread(e, held)
    else:
        held = lax.fori_loop(0, exposures, spread, held)
    row_shift, row_phase, col_phase = held
    row_out = lax.broadcasted_iota(jnp.int32, (height, depth), 0)
    tap_index = lane % height - row_out + 2 - row_shift
    row_taps = jnp.zeros((height, depth), jnp.float32)
    for k in range(TAPS):
        row_taps = jnp.where(tap_index == k, pick_phase(row_phase, table[:, k]), row_taps)
    col_taps = [pick_phase(col_phase, table[:, k]) for k in range(TAPS)]
    image = (lane // height) % 2
    rows = []
    for which in range(2):
        masked = jnp.where(image == which, row_taps, 0.0)
        rows += [masked * col_taps[k] for k in range(TAPS)]
    full = jnp.concatenate(rows, axis=0)
    high = full.astype(jnp.bfloat16)
    low = (full - high.astype(jnp.float32)).astype(jnp.bfloat16)
    return jnp.concatenate([high, low], axis=0)


def kernel(
    count, height, columns, wide, owners, rows,
    signal_ref, weight_ref, shifts_ref, phases_ref, lik_ref, best_ref,
    images, moved, coefs, chunks, partial, final,
    send_a, send_f, recv_a, send_r, recv_r, send_g, recv_g,
):
    me = lax.axis_index("vel")
    core = lax.rem(me, 2)
    chip = me // 2
    chips = count // 2
    partner = me + 1 - 2 * core

    barrier = pltpu.get_barrier_semaphore()

    def greet(d):
        pl.semaphore_signal(
            barrier, inc=1, device_id={"vel": lax.rem(me + d, count)}, device_id_type=MESH
        )

    loop(1, count, greet)
    images[me] = jnp.concatenate(
        [signal_ref[0].astype(jnp.float32), weight_ref[0].astype(jnp.float32)], axis=0
    ).astype(jnp.bfloat16)
    coefs[...] = coefficient_rows(shifts_ref, phases_ref, count, height)
    pl.semaphore_wait(barrier, count - 1)

    def block_copy(e, to, send_sem):
        return pltpu.make_async_remote_copy(
            src_ref=images.at[e], dst_ref=images.at[e], send_sem=send_sem,
            recv_sem=recv_a.at[e], device_id={"vel": to}, device_id_type=MESH,
        )

    def source(d, side):
        return lax.rem(chip + chips - d, chips) * 2 + side

    def target(d):
        return lax.rem(chip + d, chips) * 2 + core

    def place(e):
        block = images[e].astype(jnp.float32)
        block = jnp.concatenate(
            [block, jnp.zeros((2 * height, wide - columns), jnp.float32)], axis=1
        )
        amount = lax.rem(wide + 2 - shifts_ref[0, e, 1], wide)
        start = pl.multiple_of(e * 2 * height, 2 * height)
        moved[pl.ds(start, 2 * height), :] = pltpu.roll(block, amount, 1).astype(jnp.bfloat16)

    loop(1, chips, lambda d: block_copy(me, target(d), send_a.at[d]).start())
    block_copy(me, partner, send_f.at[0]).start()
    place(me)

    def relay(d):
        e = source(d, core)
        block_copy(e, partner, send_f.at[d]).wait_recv()
        block_copy(e, partner, send_f.at[d]).start()
        place(e)

    loop(1, chips, relay)

    def arrive(d):
        e = source(d, 1 - core)
        block_copy(e, partner, send_f.at[d]).wait_recv()
        place(e)

    loop(0, chips, arrive)

    acc = jnp.dot(coefs[...], moved[...], preferred_element_type=jnp.float32)
    half = 2 * TAPS * height
    acc = acc[:half] + acc[half:]
    sums = []
    for which in range(2):
        total = None
        for k in range(TAPS):
            at = (which * TAPS + k) * height
            term = acc[at : at + height]
            if k:
                term = pltpu.roll(term, wide - k, 1)
            term = term[:, :columns]
            total = term if total is None else total + term
        sums.append(total)
    likelihood = sums[0] / jnp.sqrt(jnp.maximum(sums[1], 1.0))
    lik_ref[0] = likelihood

    tiles = columns // LANES
    per_tile = height // rows
    for tile in range(tiles):
        for part in range(per_tile):
            chunks[tile * per_tile + part] = likelihood[
                part * rows : (part + 1) * rows, tile * LANES : (tile + 1) * LANES
            ]

    def chunk_copy(owner, slot, to):
        return pltpu.make_async_remote_copy(
            src_ref=chunks.at[owner], dst_ref=partial.at[slot], send_sem=send_r.at[owner],
            recv_sem=recv_r.at[slot], device_id={"vel": to}, device_id_type=MESH,
        )

    def final_copy(slot, to, send_sem):
        return pltpu.make_async_remote_copy(
            src_ref=final.at[slot], dst_ref=final.at[slot], send_sem=send_sem,
            recv_sem=recv_g.at[slot], device_id={"vel": to}, device_id_type=MESH,
        )

    whole_group = owners == count

    def send_chunk(d):
        to = lax.rem(me + d, count)
        if whole_group:
            chunk_copy(to, me, to).start()
        else:
            @pl.when(to < owners)
            def _():
                chunk_copy(to, me, to).start()

    loop(1, count, send_chunk)

    def reduce_own():
        partial[me] = chunks[me]
        loop(1, count, lambda d: chunk_copy(me, lax.rem(me + d, count), me).wait_recv())
        final[me] = jnp.max(partial[...], axis=0)
        loop(
            1, count,
            lambda d: final_copy(me, lax.rem(me + d, count), send_g.at[d]).start(),
        )

    if whole_group:
        reduce_own()
    else:
        pl.when(me < owners)(reduce_own)

    def take_final(d):
        slot = lax.rem(me + count - d, count)
        if whole_group:
            final_copy(slot, partner, send_g.at[d]).wait_recv()
        else:
            @pl.when(slot < owners)
            def _():
                final_copy(slot, partner, send_g.at[d]).wait_recv()

    loop(1, count, take_final)
    for tile in range(tiles):
        for part in range(per_tile):
            best_ref[part * rows : (part + 1) * rows, tile * LANES : (tile + 1) * LANES] = final[
                tile * per_tile + part
            ]

    loop(1, chips, lambda d: block_copy(me, target(d), send_a.at[d]).wait_send())
    loop(0, chips, lambda d: block_copy(source(d, core), partner, send_f.at[d]).wait_send())

    def sent_chunk(d):
        to = lax.rem(me + d, count)
        if whole_group:
            chunk_copy(to, me, to).wait_send()
        else:
            @pl.when(to < owners)
            def _():
                chunk_copy(to, me, to).wait_send()

    loop(1, count, sent_chunk)

    def sent_final():
        loop(
            1, count,
            lambda d: final_copy(me, lax.rem(me + d, count), send_g.at[d]).wait_send(),
        )

    if whole_group:
        sent_final()
    else:
        pl.when(me < owners)(sent_final)


def body(count, signal, weight, shifts, phases):
    height, columns = signal.shape[1], signal.shape[2]
    reach = shifts.shape[1] + 5
    wide = columns + -(-reach // LANES) * LANES
    pieces = height * columns // LANES
    rows = max(1, pieces // count)
    owners = pieces // rows
    dma = pltpu.SemaphoreType.DMA
    vmem = pl.BlockSpec(memory_space=pltpu.VMEM)
    smem = pl.BlockSpec(memory_space=pltpu.SMEM)
    return pl.pallas_call(
        functools.partial(kernel, count, height, columns, wide, owners, rows),
        out_shape=(
            jax.ShapeDtypeStruct((1, height, columns), jnp.float32),
            jax.ShapeDtypeStruct((height, columns), jnp.float32),
        ),
        in_specs=[vmem, vmem, smem, smem],
        out_specs=(vmem, vmem),
        scratch_shapes=[
            pltpu.VMEM((count, 2 * height, columns), jnp.bfloat16),
            pltpu.VMEM((count * 2 * height, wide), jnp.bfloat16),
            pltpu.VMEM((4 * TAPS * height, count * 2 * height), jnp.bfloat16),
            pltpu.VMEM((owners, rows, LANES), jnp.float32),
            pltpu.VMEM((count, rows, LANES), jnp.float32),
            pltpu.VMEM((owners, rows, LANES), jnp.float32),
            dma((count // 2,)), dma((count // 2,)), dma((count,)),
            dma((owners,)), dma((count,)), dma((count,)), dma((owners,)),
        ],
        compiler_params=pltpu.CompilerParams(collective_id=0, has_side_effects=True),
    )(signal, weight, shifts, phases)


def solution(mesh):
    part = P(("groups", "vel"), None, None)
    own = P("vel", None, None)
    return jax.shard_map(
        functools.partial(body, mesh.shape["vel"]),
        mesh=mesh,
        in_specs=(part, part, own, own),
        out_specs=(part, P("groups", None)),
        check_vma=False,
    )
```

time: 175 us -> 26.8 us (0.15)
  blocking collectives: 101 us -> 0 us
  local copies, waits for them, and re-layouts: 42.5 us -> 3.98 us
  other arithmetic: 30.8 us -> 0 us
  Pallas kernels: 0 us -> 21.9 us
    pmax x1 -> x0, blocking collectives: 59.1 us -> none  [body(): best_likelihood = lax.pmax(jnp.max(likelihood, axis=0), 'vel')]
    all_gather x2 -> x0, blocking collectives: 41.7 us -> none  [the longest x1 23.7 us: body(): lax.all_gather(weight, 'vel', axis=0, tiled=True)]
    another operation x1 -> x0, other arithmetic: 28.2 us -> none  [widen(): images = jnp.stack([signal_part, weight_part], axis=1)]
    gather x3 -> x0, local copies, waits for them, and re-layouts: 25.9 us -> none  [the longest x2 24.4 us: place_pair(): lax.dynamic_slice(padded, (anchor, anchor, col_start), (2, height, column...]
    pallas_call x0 -> x1, Pallas kernels: none -> 21.9 us  [body(): pl.pallas_call(functools.partial(kernel, count, height, columns, wide, ow...]
    another operation x2 -> x0, local copies, waits for them, and re-layouts: 15 us -> none  [widen(): images = jnp.stack([signal_part, weight_part], axis=1)]
    unnamed x7 -> x8, local copies, waits for them, and re-layouts: 1.03 us -> 3.98 us
where the time goes in v1:
time: 26.8 us; the launch traced here: 26.5 us
  Pallas kernels  21.9 us (82%)
  local copies, waits for them, and re-layouts  3.98 us (15%)
  between operations  0.66 us (2%)
    pallas_call x1, Pallas kernels, body(): pl.pallas_call(functools.partial(kernel, count, height, columns, wide, ow...  21.9 us
    unnamed x8, local copies, waits for them, and re-layouts  3.98 us

profile of v1, /device:TPU:0, one launch (start us, length us, event | category | flops | bytes accessed | tf_op | source)
XLA Modules:
  0.0 26.5 jit_solution(14694138461833860026)
XLA Ops:
  0.6 0.0 copy-start.1
  0.6 1.4 %copy.6.shifts_ref = s32[1,16,2]{2,1,0:T(8,128)} copy(s32[1,16,2]{1,2,0:T(2,128)} %param.6) | data formatting | bytes 256 | tf_op args[2]
  2.0 0.0 copy-done.1
  2.0 0.7 %copy.7.phases_ref = s32[1,16,2]{2,1,0:T(8,128)} copy(s32[1,16,2]{1,2,0:T(2,128)S(1)} %copy-done.1) | data formatting | bytes 256 | tf_op args[3]
  2.7 21.9 %shard_map.59 = (f32[1,8,512]{2,1,0:T(8,128)}, f32[8,512]{1,0:T(8,128)}) custom-call(bf16[1,8,512]{2,1,0:T(8,128)(2,1)} %signal_ref.1, bf16[1,8,512]{2,1,0:T(8,128)(2,1)} %weight_ref.1, s32[1,16,2]{2,1,0:T(8,128)} %copy.6.shifts_ref, s32[1,16,2]{2,1,0:T(8,128)} %copy.7.phases_ref), custom_call_target="tpu_custom_call" | custom-call | tf_op jit(solution)/shard_map/pallas_call | solution.py:260
  24.6 0.0 copy-start
  24.6 1.3 %copy.10 = f32[1,8,512]{2,1,0:T(8,128)} copy(f32[1,8,512]{2,1,0:T(8,128)} %get-tuple-element.4) | data formatting | bytes 32768
  25.9 0.0 copy-done
  25.9 0.6 %copy.11 = f32[8,512]{1,0:T(8,128)} copy(f32[8,512]{1,0:T(8,128)S(1)} %copy-done) | data formatting | bytes 32768
Async XLA Ops:
  0.6 1.4 %copy-start.1 = (s32[1,16,2]{1,2,0:T(2,128)S(1)}, s32[1,16,2]{1,2,0:T(2,128)}, u32[]{:S(2)}) copy-start(s32[1,16,2]{1,2,0:T(2,128)} %param.7) | copy-start | bytes 388
  24.6 1.3 %copy-start = (f32[8,512]{1,0:T(8,128)S(1)}, f32[8,512]{1,0:T(8,128)}, u32[]{:S(2)}) copy-start(f32[8,512]{1,0:T(8,128)} %get-tuple-element.5) | copy-start | bytes 49156

commit v2 on v1

v2 whole, which is shorter than its diff:
```python
import functools
import math

import jax
import jax.numpy as jnp
import numpy as np
from jax import lax
from jax.experimental import pallas as pl
from jax.experimental.pallas import tpu as pltpu
from jax.sharding import PartitionSpec as P

TAPS = 6
PHASES = 8
LANES = 128
MESH = pl.DeviceIdType.MESH


def tap_table():
    distance = (np.arange(TAPS)[None, :] - 2) - np.arange(PHASES)[:, None] / 8.0
    raw = np.sinc(distance) * np.sinc(distance / 3.0)
    return (raw / raw.sum(axis=1, keepdims=True)).astype(np.float32)


def loop(start, stop, step):
    if stop - start <= 16:
        for at in range(start, stop):
            step(at)
    else:
        lax.fori_loop(start, stop, lambda at, c: (step(at), c)[1], 0)


def pick_phase(phase, column):
    value = jnp.full(phase.shape, float(column[0]), jnp.float32)
    for at in range(1, PHASES):
        value = jnp.where(phase == at, float(column[at]), value)
    return value


def coefficient_rows(shifts_ref, phases_ref, exposures, height):
    depth = exposures * 2 * height
    table = tap_table()
    lane = lax.broadcasted_iota(jnp.int32, (1, depth), 1)
    owner = lane // (2 * height)

    def spread(e, held):
        row_shift, row_phase, col_phase = held
        here = owner == e
        return (
            jnp.where(here, shifts_ref[0, 0, e], row_shift),
            jnp.where(here, phases_ref[0, 0, e], row_phase),
            jnp.where(here, phases_ref[0, 1, e], col_phase),
        )

    held = (jnp.zeros((1, depth), jnp.int32),) * 3
    if exposures <= 16:
        for e in range(exposures):
            held = spread(e, held)
    else:
        held = lax.fori_loop(0, exposures, spread, held)
    row_shift, row_phase, col_phase = held
    row_out = lax.broadcasted_iota(jnp.int32, (height, depth), 0)
    tap_index = lane % height - row_out + 2 - row_shift
    row_taps = jnp.zeros((height, depth), jnp.float32)
    for k in range(TAPS):
        row_taps = jnp.where(tap_index == k, pick_phase(row_phase, table[:, k]), row_taps)
    col_taps = [pick_phase(col_phase, table[:, k]) for k in range(TAPS)]
    image = (lane // height) % 2
    rows = []
    for which in range(2):
        masked = jnp.where(image == which, row_taps, 0.0)
        rows += [masked * col_taps[k] for k in range(TAPS)]
    full = jnp.concatenate(rows, axis=0)
    high = full.astype(jnp.bfloat16)
    low = (full - high.astype(jnp.float32)).astype(jnp.bfloat16)
    return jnp.concatenate([high, low], axis=0)


def kernel(
    count, height, columns, wide,
    signal_hbm, weight_hbm, shifts_hbm, phases_hbm, lik_hbm, best_hbm,
    own, shifts_ref, phases_ref, images, moved, coefs, lik, halves, pair_in, gathered, best,
    send_a, send_f, recv_a, send_g, recv_g, pair_sem, last_sem, load_sem, store_sem,
):
    me = lax.axis_index("vel")
    core = lax.rem(me, 2)
    chip = me // 2
    chips = count // 2
    partner = me + 1 - 2 * core
    half = columns // 2

    loads = [
        pltpu.make_async_copy(signal_hbm.at[0], own.at[0], load_sem.at[0]),
        pltpu.make_async_copy(weight_hbm.at[0], own.at[1], load_sem.at[1]),
        pltpu.make_async_copy(shifts_hbm, shifts_ref, load_sem.at[2]),
        pltpu.make_async_copy(phases_hbm, phases_ref, load_sem.at[3]),
    ]
    for copy in loads:
        copy.start()

    def source(d, side):
        return lax.rem(chip + chips - d, chips) * 2 + side

    def target(d):
        return lax.rem(chip + d, chips) * 2 + core

    barrier = pltpu.get_barrier_semaphore()

    def greet(to):
        pl.semaphore_signal(barrier, inc=1, device_id={"vel": to}, device_id_type=MESH)

    loop(1, chips, lambda d: greet(target(d)))
    greet(partner)
    for copy in loads:
        copy.wait()
    images[me] = jnp.concatenate(
        [own[0].astype(jnp.float32), own[1].astype(jnp.float32)], axis=0
    ).astype(jnp.bfloat16)
    coefs[...] = coefficient_rows(shifts_ref, phases_ref, count, height)
    pl.semaphore_wait(barrier, chips)

    def block_copy(e, to, send_sem):
        return pltpu.make_async_remote_copy(
            src_ref=images.at[e], dst_ref=images.at[e], send_sem=send_sem,
            recv_sem=recv_a.at[e], device_id={"vel": to}, device_id_type=MESH,
        )

    def place(e):
        block = images[e].astype(jnp.float32)
        block = jnp.concatenate(
            [block, jnp.zeros((2 * height, wide - columns), jnp.float32)], axis=1
        )
        amount = lax.rem(wide + 2 - shifts_ref[0, 1, e], wide)
        start = pl.multiple_of(e * 2 * height, 2 * height)
        moved[pl.ds(start, 2 * height), :] = pltpu.roll(block, amount, 1).astype(jnp.bfloat16)

    loop(1, chips, lambda d: block_copy(me, target(d), send_a.at[d]).start())
    block_copy(me, partner, send_f.at[0]).start()
    place(me)

    def relay(d):
        e = source(d, core)
        block_copy(e, partner, send_f.at[d]).wait_recv()
        block_copy(e, partner, send_f.at[d]).start()
        place(e)

    loop(1, chips, relay)

    def arrive(d):
        e = source(d, 1 - core)
        block_copy(e, partner, send_f.at[d]).wait_recv()
        place(e)

    loop(0, chips, arrive)

    acc = jnp.dot(coefs[...], moved[...], preferred_element_type=jnp.float32)
    size = 2 * TAPS * height
    acc = acc[:size] + acc[size:]
    sums = []
    for which in range(2):
        total = None
        for k in range(TAPS):
            at = (which * TAPS + k) * height
            term = acc[at : at + height]
            if k:
                term = pltpu.roll(term, wide - k, 1)
            term = term[:, :columns]
            total = term if total is None else total + term
        sums.append(total)
    likelihood = sums[0] / jnp.sqrt(jnp.maximum(sums[1], 1.0))
    halves[0] = likelihood[:, :half]
    halves[1] = likelihood[:, half:]
    lik[...] = likelihood

    def pair_copy(src, dst, sems):
        return pltpu.make_async_remote_copy(
            src_ref=src, dst_ref=dst, send_sem=sems.at[0], recv_sem=sems.at[1],
            device_id={"vel": partner}, device_id_type=MESH,
        )

    exchange = pair_copy(halves.at[1 - core], pair_in, pair_sem)
    exchange.start()
    store_lik = pltpu.make_async_copy(lik, lik_hbm.at[0], store_sem.at[0])
    store_lik.start()
    exchange.wait_recv()
    gathered[chip] = jnp.maximum(halves[core], pair_in[...])

    def gather_copy(slot, to, d):
        return pltpu.make_async_remote_copy(
            src_ref=gathered.at[slot], dst_ref=gathered.at[slot], send_sem=send_g.at[d],
            recv_sem=recv_g.at[slot], device_id={"vel": to}, device_id_type=MESH,
        )

    loop(1, chips, lambda d: gather_copy(chip, target(d), d).start())
    loop(1, chips, lambda d: gather_copy(source(d, 0) // 2, partner, d).wait_recv())
    best[core] = jnp.max(gathered[...], axis=0)
    share = pair_copy(best.at[core], best.at[core], last_sem)
    share.start()
    share.wait_recv()
    stores = [
        pltpu.make_async_copy(
            best.at[side], best_hbm.at[:, side * half : (side + 1) * half], store_sem.at[1 + side]
        )
        for side in range(2)
    ]
    for copy in stores:
        copy.start()
    loop(1, chips, lambda d: block_copy(me, target(d), send_a.at[d]).wait_send())
    loop(0, chips, lambda d: block_copy(source(d, core), partner, send_f.at[d]).wait_send())
    loop(1, chips, lambda d: gather_copy(chip, target(d), d).wait_send())
    exchange.wait_send()
    share.wait_send()
    store_lik.wait()
    for copy in stores:
        copy.wait()


def body(count, signal, weight, shifts, phases):
    height, columns = signal.shape[1], signal.shape[2]
    exposures = shifts.shape[1]
    reach = exposures + 5
    wide = columns + -(-reach // LANES) * LANES
    half = columns // 2
    chips = count // 2
    dma = pltpu.SemaphoreType.DMA
    hbm = pl.BlockSpec(memory_space=pl.ANY)
    return pl.pallas_call(
        functools.partial(kernel, count, height, columns, wide),
        out_shape=(
            jax.ShapeDtypeStruct((1, height, columns), jnp.float32),
            jax.ShapeDtypeStruct((height, columns), jnp.float32),
        ),
        in_specs=[hbm] * 4,
        out_specs=(hbm, hbm),
        scratch_shapes=[
            pltpu.VMEM((2, height, columns), jnp.bfloat16),
            pltpu.SMEM((1, 2, exposures), jnp.int32),
            pltpu.SMEM((1, 2, exposures), jnp.int32),
            pltpu.VMEM((count, 2 * height, columns), jnp.bfloat16),
            pltpu.VMEM((count * 2 * height, wide), jnp.bfloat16),
            pltpu.VMEM((4 * TAPS * height, count * 2 * height), jnp.bfloat16),
            pltpu.VMEM((height, columns), jnp.float32),
            pltpu.VMEM((2, height, half), jnp.float32),
            pltpu.VMEM((height, half), jnp.float32),
            pltpu.VMEM((chips, height, half), jnp.float32),
            pltpu.VMEM((2, height, half), jnp.float32),
            dma((chips,)), dma((chips,)), dma((count,)),
            dma((chips,)), dma((chips,)), dma((2,)), dma((2,)), dma((4,)), dma((3,)),
        ],
        compiler_params=pltpu.CompilerParams(collective_id=0, has_side_effects=True),
    )(signal, weight, jnp.swapaxes(shifts, 1, 2), jnp.swapaxes(phases, 1, 2))


def solution(mesh):
    part = P(("groups", "vel"), None, None)
    own = P("vel", None, None)
    return jax.shard_map(
        functools.partial(body, mesh.shape["vel"]),
        mesh=mesh,
        in_specs=(part, part, own, own),
        out_specs=(part, P("groups", None)),
        check_vma=False,
    )
```

time: 26.8 us -> 22.3 us (0.83)
  the two profiles are of different devices: /device:TPU:0 before, /device:TPU:1 now
where the time goes in v2:
time: 22.3 us; the launch traced here: 22 us
  Pallas kernels  19.5 us (87%)
  local copies, waits for them, and re-layouts  1.94 us (9%)
  between operations  0.65 us (3%)
    pallas_call x1, Pallas kernels, body(): pl.pallas_call(functools.partial(kernel, count, height, columns, wide), o...  19.5 us
    unnamed x4, local copies, waits for them, and re-layouts  1.94 us

profile of v2, /device:TPU:1, one launch (start us, length us, event | category | flops | bytes accessed | tf_op | source)
XLA Modules:
  0.0 22.0 jit_solution(18269404600649226832)
XLA Ops:
  0.6 19.5 %shard_map.59 = (f32[1,8,512]{2,1,0:T(8,128)}, f32[8,512]{1,0:T(8,128)}) custom-call(bf16[1,8,512]{2,1,0:T(8,128)(2,1)} %signal_hbm.1, bf16[1,8,512]{2,1,0:T(8,128)(2,1)} %weight_hbm.1, s32[1,2,16]{2,1,0:T(2,128)} %bitcast.2, s32[1,2,16]{2,1,0:T(2,128)} %bitcast.3), custom_call_target="tpu_custom_call" | custom-call | tf_op jit(solution)/shard_map/pallas_call | solution.py:226
  20.1 0.0 copy-start
  20.1 1.3 %copy.8 = f32[1,8,512]{2,1,0:T(8,128)} copy(f32[1,8,512]{2,1,0:T(8,128)} %get-tuple-element.4) | data formatting | bytes 32768
  21.4 0.0 copy-done
  21.4 0.6 %copy.9 = f32[8,512]{1,0:T(8,128)} copy(f32[8,512]{1,0:T(8,128)S(1)} %copy-done) | data formatting | bytes 32768
Async XLA Ops:
  20.1 1.3 %copy-start = (f32[8,512]{1,0:T(8,128)S(1)}, f32[8,512]{1,0:T(8,128)}, u32[]{:S(2)}) copy-start(f32[8,512]{1,0:T(8,128)} %get-tuple-element.5) | copy-start | bytes 49156
